TPU v7x, 32 devices: a whole 2x2x4 slice. The times are simulated.
32 devices in a mesh: dom: 2 (over x), tok: 16 (over z, y, core).
Axes of the slice: x: 2, y: 2, z: 4, core: 2. Of those that a mesh axis runs over, the one named last changes fastest.
Arguments:
- tokens: bfloat16 [512, 4096], P(('dom', 'tok')), parts along dimension 0, may hold values from -6 to 6
- rotation_flip: int32 [4096], replicated, may hold values from 0 to 1
- gate_up: bfloat16 [4, 4096, 16384], P('dom', None, 'tok'), parts along dimension 0, may hold values from -0.09375 to 0.09375
- quant_codes: bfloat16 [4, 4096, 16384], P('dom', None, 'tok'), parts along dimension 0, may hold values from -7 to 7
- quant_exps: int32 [4, 32, 16384], P('dom', None, 'tok'), parts along dimension 0, may hold values from -10 to -7
- down_rows: bfloat16 [32768, 4096], P(('dom', 'tok')), parts along dimension 0, may hold values from -0.046875 to 0.046875
Outputs:
- correction: bfloat16 [32768, 4096], P(('dom', 'tok')), parts along dimension 0
There are 2 independent parts, one for each index of `dom`. A program takes and returns all parts, laid end to end along the dimension named above; an argument that names none is the same for every part. Nothing has to cross between parts.
All inputs are finite; a program needn't handle non-finite values.
Results may differ from a plain program's by a relative error of at most 0.012.
Values may be sent and summed in bfloat16 or wider, within the bound.
No kernel may reach another device: no remote copies, remote signals or barrier semaphores. Data moves between devices by JAX's collectives and lax.ppermute only.
A program may use at most 128 MiB of HBM per device.

v0:
```python
import jax
import jax.numpy as jnp
from jax import lax
from jax.sharding import PartitionSpec as P


def hadamard_table(order):
    index = jnp.arange(order, dtype=jnp.int32)
    common = index[:, None] & index[None, :]
    parity = jnp.zeros((order, order), jnp.int32)
    for bit_pos in range(max(order.bit_length() - 1, 1)):
        parity = parity ^ common >> bit_pos & 1
    return (1 - 2 * parity).astype(jnp.float32)


def rotate(inputs, flip):
    width = inputs.shape[-1]
    signed = inputs.astype(jnp.float32) * (1 - 2 * flip).astype(jnp.float32)
    power = width.bit_length() - 1
    outer_len = 2 ** (power // 2)
    inner_len = width // outer_len
    blocks = signed.reshape(-1, outer_len, inner_len)
    mixed = jnp.einsum(
        "ab,nbc,cd->nad",
        hadamard_table(outer_len),
        blocks,
        hadamard_table(inner_len),
        precision=lax.Precision.HIGHEST,
    )
    return (mixed.reshape(-1, width) * (1.0 / width**0.5)).astype(jnp.bfloat16)


def dequant(codes, exps):
    groups = exps.shape[1]
    scales = jnp.exp2(exps.astype(jnp.float32))
    shaped = codes.astype(jnp.float32).reshape(2, groups, codes.shape[1] // groups, codes.shape[2])
    return (shaped * scales[:, :, None, :]).reshape(codes.shape).astype(jnp.bfloat16)


def swiglu(inputs, weights):
    gate = jnp.dot(inputs, weights[0], preferred_element_type=jnp.float32)
    upper = jnp.dot(inputs, weights[1], preferred_element_type=jnp.float32)
    return (jax.nn.silu(gate) * upper).astype(jnp.bfloat16)


def per_device(tokens, rotation_flip, gate_up, quant_codes, quant_exps, down_rows):
    quant_weight = dequant(quant_codes, quant_exps)
    piece = lax.all_gather(tokens, "tok", axis=0, tiled=True)
    hid_full = swiglu(piece, gate_up)
    hid_quant = swiglu(rotate(piece, rotation_flip), quant_weight)
    mismatch = (hid_full.astype(jnp.float32) - hid_quant.astype(jnp.float32)).astype(jnp.bfloat16)
    total_tokens = mismatch.shape[0]
    partial_proj = jnp.dot(mismatch, down_rows, preferred_element_type=jnp.float32)
    projected = lax.psum(partial_proj, "tok").astype(jnp.bfloat16)
    gram = lax.dot_general(
        hid_quant, projected, (((0,), (0,)), ((), ())), preferred_element_type=jnp.float32
    )
    return (gram * (1.0 / total_tokens**0.5)).astype(jnp.bfloat16)


def solution(mesh):
    placed = (
        P(("dom", "tok"), None),
        P(),
        P("dom", None, "tok"),
        P("dom", None, "tok"),
        P("dom", None, "tok"),
        P(("dom", "tok"), None),
    )
    return jax.shard_map(
        per_device, mesh=mesh, in_specs=placed, out_specs=P(("dom", "tok"), None), check_vma=False
    )
```

profile of v0, /device:TPU:1, one launch (start us, length us, event | category | flops | bytes accessed | tf_op | source)
XLA Modules:
  0.0 203.8 jit_solution(15538142856855820026)
XLA Ops:
  6.5 0.0 all-gather.2.cloned.1.call-start
  6.5 0.7 all-gather.2.cloned.1.call-update
  7.3 1.0 multiply_exponential_fusion
  8.3 0.0 copy-start.2
  8.3 14.8 %fusion = bf16[2,4096,1024]{2,1,0:T(8,128)(2,1)} fusion(bf16[2,4096,1024]{2,1,0:T(8,128)(2,1)} %param.9, f32[2,32,1024]{2,1,0:T(8,128)S(1)} %multiply_exponential_fusion), kind=kLoop, calls=%fused_computation.1 | loop fusion | flops 25165824 | bytes 33816576 | tf_op jit(solution)/shard_map/convert_element_type | solution.py:37
  23.1 0.0 copy-done.2
  23.1 30.4 %all-gather.2.cloned.1.call-done = bf16[256,4096]{1,0:T(8,128)(2,1)} async-done(((bf16[16,4096]{1,0:T(8,128)(2,1)}), bf16[256,4096]{1,0:T(8,128)(2,1)}) %all-gather.2.cloned.1.call-update) | async-done | bytes 2097168 | tf_op jit(solution)/shard_map/all_gather | solution.py:48
  53.4 3.3 %copy.8 = bf16[256,4096]{0,1:T(8,128)(2,1)S(1)} copy(bf16[256,4096]{1,0:T(8,128)(2,1)} %all-gather.2.cloned.1.call-done) | data formatting | bytes 4194304 | tf_op jit(solution)/shard_map/all_gather | solution.py:48
  56.7 0.0 copy-start
  56.7 0.7 convert_multiply_fusion
  57.5 6.8 %fusion.11 = f32[256,64,64]{0,2,1:T(8,128)S(1)} fusion(f32[256,64,64]{0,2,1:T(8,128)S(1)} %bitcast.47), kind=kOutput, calls=%fused_computation.15 | convolution fusion | flops 805392384 | bytes 8388608 | tf_op jit(solution)/shard_map/ab,nbc,cd->nad/dot_general | solution.py:23
  64.2 6.0 %multiply_convert_fusion.1 = bf16[256,64,64]{0,2,1:T(8,128)(2,1)S(1)} fusion(f32[256,64,64]{0,2,1:T(8,128)S(1)} %fusion.11), kind=kOutput, calls=%fused_computation.17 | convolution fusion | flops 807489536 | bytes 6291456 | tf_op jit(solution)/shard_map/ab,nbc,cd->nad/dot_general | solution.py:23
  70.3 0.0 copy-done
  70.3 2.4 %fusion.2 = f32[256,1024]{1,0:T(8,128)S(1)} fusion(bf16[256,4096]{0,1:T(8,128)(2,1)S(1)} %bitcast.48, bf16[2,4096,1024]{2,1,0:T(8,128)(2,1)S(1)} %copy-done), kind=kOutput, calls=%fused_computation.6 | convolution fusion | flops 2147483648 | bytes 11534336 | tf_op jit(solution)/shard_map/dot_general | solution.py:41
  72.6 0.0 copy-start.1
  72.6 2.4 %fusion.20 = bf16[256,1024]{1,0:T(8,128)(2,1)S(1)} fusion(bf16[256,4096]{0,1:T(8,128)(2,1)S(1)} %bitcast.49, bf16[2,4096,1024]{2,1,0:T(8,128)(2,1)S(1)} %copy-done, f32[256,1024]{1,0:T(8,128)S(1)} %fusion.2), kind=kOutput, calls=%fused_computation.22 | convolution fusion | flops 2149056512 | bytes 12058624 | tf_op jit(solution)/shard_map/dot_general | solution.py:42
  75.1 0.0 copy-done.1
  75.1 6.7 %fusion.5 = f32[256,1024]{1,0:T(8,128)} fusion(bf16[256,4096]{1,0:T(8,128)(2,1)S(1)} %copy-done.1, bf16[2,4096,1024]{2,1,0:T(8,128)(2,1)} %param.8), kind=kOutput, calls=%fused_computation.9 | convolution fusion | flops 2147483648 | bytes 11534336 | tf_op jit(solution)/shard_map/dot_general | solution.py:41
  81.8 12.7 %fusion.34 = f32[256,4096]{1,0:T(8,128)} fusion(bf16[1024,4096]{1,0:T(8,128)(2,1)} %param.11, bf16[256,4096]{1,0:T(8,128)(2,1)S(1)} %copy-done.1, bf16[2,4096,1024]{2,1,0:T(8,128)(2,1)} %param.8, bf16[256,1024]{1,0:T(8,128)(2,1)S(1)} %fusion.20, f32[256,1024]{1,0:T(8,128)} %fusion.5), kind=kOutput, calls=%fused_computation.27 | convolution fusion | flops 4297588736 | bytes 24641536 | tf_op jit(solution)/shard_map/dot_general | solution.py:53
  94.5 96.6 %all-reduce.1 = bf16[256,4096]{1,0:T(8,128)(2,1)S(1)} all-reduce(f32[256,4096]{1,0:T(8,128)} %fusion.34), channel_id=1, replica_groups=mesh['dom'=2,'tok'=16] {'tok'}, use_global_device_ids=true, to_apply=%region_0.1 | all-reduce | flops 1048576 | bytes 6291456 | tf_op jit(solution)/shard_map/psum | solution.py:54
  191.1 5.8 %multiply_convert_fusion = bf16[1024,4096]{1,0:T(8,128)(2,1)} fusion(bf16[256,1024]{1,0:T(8,128)(2,1)S(1)} %fusion.20, bf16[256,4096]{1,0:T(8,128)(2,1)S(1)} %all-reduce.1), kind=kOutput, calls=%fused_computation.2 | convolution fusion | flops 2155872256 | bytes 11010048 | tf_op jit(solution)/shard_map/dot_general | solution.py:55
  (1 shorter events, 0.0 us)
Async XLA Ops:
  6.5 46.9 %all-gather.2.cloned.1.call-start = ((), (), s32[]{:S(2)}) async-start(), calls=%async_computation | async-start | bytes 2228224 | tf_op jit(solution)/shard_map/all_gather | solution.py:48
  8.3 14.8 %copy-start.2 = (s32[4096]{0:T(1024)S(1)}, s32[4096]{0:T(1024)}, u32[]{:S(2)}) copy-start(s32[4096]{0:T(1024)} %param.7) | copy-start | bytes 49156
  56.7 13.6 %copy-start = (bf16[2,4096,1024]{2,1,0:T(8,128)(2,1)S(1)}, bf16[2,4096,1024]{2,1,0:T(8,128)(2,1)}, u32[]{:S(2)}) copy-start(bf16[2,4096,1024]{2,1,0:T(8,128)(2,1)} %fusion) | copy-start | bytes 50331652
  72.6 2.5 %copy-start.1 = (bf16[256,4096]{1,0:T(8,128)(2,1)S(1)}, bf16[256,4096]{1,0:T(8,128)(2,1)}, u32[]{:S(2)}) copy-start(bf16[256,4096]{1,0:T(8,128)(2,1)} %all-gather.2.cloned.1.call-done) | copy-start | bytes 6291460
Sparse Core Ops, SparseCore 0:
  9.5 43.9 all-gather.1
where the time goes:
time: 204 us
  blocking collectives  96.6 us (47%)
  matrix products  42.8 us (21%)
  waiting for transfers between devices  31.1 us (15%)
  other arithmetic  16.5 us (8%)
  between operations  13.5 us (7%)
  local copies, waits for them, and re-layouts  3.28 us (2%)
    psum x1, blocking collectives, per_device(): projected = lax.psum(partial_proj, 'tok').astype(jnp.bfloat16)  96.6 us
    all_gather x1, waiting for transfers between devices, per_device(): piece = lax.all_gather(tokens, 'tok', axis=0, tiled=True)  30.4 us
    convert_element_type x1, other arithmetic, dequant(): (shaped * scales[:, :, None, :]).reshape(codes.shape).astype(jnp.bfloat16)  14.8 us
    dot_general x2, matrix products, rotate(): jnp.einsum('ab,nbc,cd->nad', hadamard_table(outer_len), blocks, hadamard_...  12.8 us
    dot_general x1, matrix products, per_device(): jnp.dot(mismatch, down_rows, preferred_element_type=jnp.float32)  12.7 us
    dot_general x2, matrix products, swiglu(): gate = jnp.dot(inputs, weights[0], preferred_element_type=jnp.float32)  9.03 us
    dot_general x1, matrix products, per_device(): lax.dot_general(hid_quant, projected, (((0,), (0,)), ((), ())), preferred...  5.79 us
  transfers between devices with their start and end apart: 1, of which 1 were waited for; matrix products, arithmetic and copies ran while one was open for 8% of the time, Pallas kernels for 0%

commit v1 on v0

--- a/solution.py
+++ b/solution.py
@@ -45,7 +45,20 @@
 
 def per_device(tokens, rotation_flip, gate_up, quant_codes, quant_exps, down_rows):
     quant_weight = dequant(quant_codes, quant_exps)
-    piece = lax.all_gather(tokens, "tok", axis=0, tiled=True)
+
+    def open_runs(matrix):
+        lanes = jax.lax.axis_size("tok")
+        val = sorted(((rr, (rr + 1) % lanes) for rr in range(lanes)))
+        oldest = matrix
+        store = [oldest]
+        for w in range(1, lanes):
+            oldest = jax.lax.ppermute(oldest, "tok", val)
+            store.insert(0, oldest)
+        base_arr = jnp.concatenate(store, axis=0)
+        y_new = jax.lax.axis_index("tok") + 1
+        return jnp.roll(base_arr, y_new * matrix.shape[0], axis=0)
+
+    piece = open_runs(tokens)
     hid_full = swiglu(piece, gate_up)
     hid_quant = swiglu(rotate(piece, rotation_flip), quant_weight)
     mismatch = (hid_full.astype(jnp.float32) - hid_quant.astype(jnp.float32)).astype(jnp.bfloat16)

time: 204 us -> 315 us (1.54); the launches traced: 204 us -> 311 us
  local copies, waits for them, and re-layouts: 3.28 us -> 57.7 us
  waiting for transfers between devices: 31.1 us -> 78.3 us
  between operations: 13.5 us -> 0.31 us
  starting transfers between devices: 0.01 us -> 7.47 us
  blocking collectives: 96.6 us -> 102 us
  matrix products: 42.8 us -> 46.3 us
    ppermute x0 -> x15, waiting for transfers between devices: none -> 78.3 us  [open_runs(): oldest = jax.lax.ppermute(oldest, 'tok', val)]
    concatenate x0 -> x1, local copies, waits for them, and re-layouts: none -> 32.3 us  [open_runs(): return jnp.roll(base_arr, y_new * matrix.shape[0], axis=0)]
    all_gather x1 -> x0, waiting for transfers between devices: 30.4 us -> none  [per_device(): piece = lax.all_gather(tokens, 'tok', axis=0, tiled=True)]
    ppermute x0 -> x15, local copies, waits for them, and re-layouts: none -> 23.9 us  [open_runs(): oldest = jax.lax.ppermute(oldest, 'tok', val)]
    ppermute x0 -> x15, starting transfers between devices: none -> 7.47 us  [open_runs(): oldest = jax.lax.ppermute(oldest, 'tok', val)]
    dot_general x1 -> x2, matrix products: 2.44 us -> 8.32 us  [swiglu(): upper = jnp.dot(inputs, weights[1], preferred_element_type=jnp.float32)]
    psum x1, blocking collectives: 96.6 us -> 102 us  [per_device(): projected = lax.psum(partial_proj, 'tok').astype(jnp.bfloat16)]
    all_gather x1 -> x0, local copies, waits for them, and re-layouts: 3.27 us -> none  [per_device(): piece = lax.all_gather(tokens, 'tok', axis=0, tiled=True)]
  transfers between devices with their start and end apart: 1 -> 15, of which waited for: 1 -> 13; matrix products, arithmetic and copies ran while one was open for 8% -> 13% of each run, Pallas kernels for 0% -> 0%
where the time goes in v1:
time: 315 us; the launch traced here: 311 us
  blocking collectives  102 us (32%)
  waiting for transfers between devices  78.3 us (25%)
  local copies, waits for them, and re-layouts  57.7 us (18%)
  matrix products  46.3 us (15%)
  other arithmetic  18.5 us (6%)
  starting transfers between devices  7.47 us (2%)
    psum x1, blocking collectives, per_device(): projected = lax.psum(partial_proj, 'tok').astype(jnp.bfloat16)  102 us
    ppermute x15, waiting for transfers between devices, open_runs(): oldest = jax.lax.ppermute(oldest, 'tok', val)  78.3 us
    concatenate x1, local copies, waits for them, and re-layouts, open_runs(): return jnp.roll(base_arr, y_new * matrix.shape[0], axis=0)  32.3 us
    ppermute x15, local copies, waits for them, and re-layouts, open_runs(): oldest = jax.lax.ppermute(oldest, 'tok', val)  23.9 us
    convert_element_type x1, other arithmetic, dequant(): (shaped * scales[:, :, None, :]).reshape(codes.shape).astype(jnp.bfloat16)  14.8 us
    dot_general x1, matrix products, per_device(): jnp.dot(mismatch, down_rows, preferred_element_type=jnp.float32)  13.5 us
    dot_general x2, matrix products, rotate(): jnp.einsum('ab,nbc,cd->nad', hadamard_table(outer_len), blocks, hadamard_...  12.8 us
    dot_general x2, matrix products, swiglu(): upper = jnp.dot(inputs, weights[1], preferred_element_type=jnp.float32)  8.32 us
  transfers between devices with their start and end apart: 15, of which 13 were waited for; matrix products, arithmetic and copies ran while one was open for 13% of the time, Pallas kernels for 0%

profile of v1, /device:TPU:1, one launch (start us, length us, event | category | flops | bytes accessed | tf_op | source)
XLA Modules:
  0.0 310.8 jit_solution(4147636821163713226)
XLA Ops:
  0.0 2.6 collective-permute-start
  2.6 2.3 collective-permute-done
  4.9 2.3 collective-permute-start.1
  9.2 2.4 collective-permute-start.2
  11.6 4.7 %collective-permute-done.2 = bf16[16,4096]{1,0:T(8,128)(2,1)S(1)} collective-permute-done((bf16[16,4096]{1,0:T(8,128)(2,1)S(1)}, bf16[16,4096]{1,0:T(8,128)(2,1)S(1)}, u32[]{:S(2)}, u32[]{:S(2)}) %collective-permute-start.2) | collective-permute-done | bytes 131104 | tf_op jit(solution)/shard_map/ppermute | solution.py:55
  16.3 7.1 %collective-permute-done.3 = bf16[16,4096]{1,0:T(8,128)(2,1)S(1)} collective-permute-done((bf16[16,4096]{1,0:T(8,128)(2,1)S(1)}, bf16[16,4096]{1,0:T(8,128)(2,1)S(1)}, u32[]{:S(2)}, u32[]{:S(2)}) %collective-permute-start.3) | collective-permute-done | bytes 131104 | tf_op jit(solution)/shard_map/ppermute | solution.py:55
  23.4 7.1 %collective-permute-done.4 = bf16[16,4096]{1,0:T(8,128)(2,1)S(1)} collective-permute-done((bf16[16,4096]{1,0:T(8,128)(2,1)S(1)}, bf16[16,4096]{1,0:T(8,128)(2,1)S(1)}, u32[]{:S(2)}, u32[]{:S(2)}) %collective-permute-start.4) | collective-permute-done | bytes 131104 | tf_op jit(solution)/shard_map/ppermute | solution.py:55
  30.5 7.1 %collective-permute-done.5 = bf16[16,4096]{1,0:T(8,128)(2,1)S(1)} collective-permute-done((bf16[16,4096]{1,0:T(8,128)(2,1)S(1)}, bf16[16,4096]{1,0:T(8,128)(2,1)S(1)}, u32[]{:S(2)}, u32[]{:S(2)}) %collective-permute-start.5) | collective-permute-done | bytes 131104 | tf_op jit(solution)/shard_map/ppermute | solution.py:55
  37.6 7.1 %collective-permute-done.6 = bf16[16,4096]{1,0:T(8,128)(2,1)S(1)} collective-permute-done((bf16[16,4096]{1,0:T(8,128)(2,1)S(1)}, bf16[16,4096]{1,0:T(8,128)(2,1)S(1)}, u32[]{:S(2)}, u32[]{:S(2)}) %collective-permute-start.6) | collective-permute-done | bytes 131104 | tf_op jit(solution)/shard_map/ppermute | solution.py:55
  44.7 7.1 %collective-permute-done.7 = bf16[16,4096]{1,0:T(8,128)(2,1)S(1)} collective-permute-done((bf16[16,4096]{1,0:T(8,128)(2,1)S(1)}, bf16[16,4096]{1,0:T(8,128)(2,1)S(1)}, u32[]{:S(2)}, u32[]{:S(2)}) %collective-permute-start.7) | collective-permute-done | bytes 131104 | tf_op jit(solution)/shard_map/ppermute | solution.py:55
  51.7 7.1 %collective-permute-done.8 = bf16[16,4096]{1,0:T(8,128)(2,1)S(1)} collective-permute-done((bf16[16,4096]{1,0:T(8,128)(2,1)S(1)}, bf16[16,4096]{1,0:T(8,128)(2,1)S(1)}, u32[]{:S(2)}, u32[]{:S(2)}) %collective-permute-start.8) | collective-permute-done | bytes 131104 | tf_op jit(solution)/shard_map/ppermute | solution.py:55
  58.8 7.1 %collective-permute-done.9 = bf16[16,4096]{1,0:T(8,128)(2,1)S(1)} collective-permute-done((bf16[16,4096]{1,0:T(8,128)(2,1)S(1)}, bf16[16,4096]{1,0:T(8,128)(2,1)S(1)}, u32[]{:S(2)}, u32[]{:S(2)}) %collective-permute-start.9) | collective-permute-done | bytes 131104 | tf_op jit(solution)/shard_map/ppermute | solution.py:55
  65.9 7.1 %collective-permute-done.10 = bf16[16,4096]{1,0:T(8,128)(2,1)S(1)} collective-permute-done((bf16[16,4096]{1,0:T(8,128)(2,1)S(1)}, bf16[16,4096]{1,0:T(8,128)(2,1)S(1)}, u32[]{:S(2)}, u32[]{:S(2)}) %collective-permute-start.10) | collective-permute-done | bytes 131104 | tf_op jit(solution)/shard_map/ppermute | solution.py:55
  73.0 7.1 %collective-permute-done.11 = bf16[16,4096]{1,0:T(8,128)(2,1)S(1)} collective-permute-done((bf16[16,4096]{1,0:T(8,128)(2,1)S(1)}, bf16[16,4096]{1,0:T(8,128)(2,1)S(1)}, u32[]{:S(2)}, u32[]{:S(2)}) %collective-permute-start.11) | collective-permute-done | bytes 131104 | tf_op jit(solution)/shard_map/ppermute | solution.py:55
  81.6 5.6 %collective-permute-done.12 = bf16[16,4096]{1,0:T(8,128)(2,1)S(1)} collective-permute-done((bf16[16,4096]{1,0:T(8,128)(2,1)S(1)}, bf16[16,4096]{1,0:T(8,128)(2,1)S(1)}, u32[]{:S(2)}, u32[]{:S(2)}) %collective-permute-start.12) | collective-permute-done | bytes 131104 | tf_op jit(solution)/shard_map/ppermute | solution.py:55
  88.3 14.8 %fusion = bf16[2,4096,1024]{2,1,0:T(8,128)(2,1)} fusion(bf16[2,4096,1024]{2,1,0:T(8,128)(2,1)} %param.9, f32[2,32,1024]{2,1,0:T(8,128)S(1)} %multiply_exponential_fusion), kind=kLoop, calls=%fused_computation.1 | loop fusion | flops 25165824 | bytes 33816576 | tf_op jit(solution)/shard_map/convert_element_type | solution.py:37
  106.8 2.3 copy.20
  109.1 2.2 copy.19
  115.5 2.2 copy.15
  117.7 2.3 copy.14
  122.6 2.2 copy.11
  124.9 2.2 copy.10
  127.1 32.3 %concatenate.6 = bf16[512,4096]{0,1:T(8,128)(2,1)} concatenate(bf16[16,4096]{0,1:T(8,128)(2,1)} %copy.10, bf16[16,4096]{0,1:T(8,128)(2,1)} %copy.11, bf16[16,4096]{0,1:T(8,128)(2,1)} %copy.12, bf16[16,4096]{0,1:T(8,128)(2,1)} %copy.13, bf16[16,4096]{0,1:T(8,128)(2,1)} %copy.14, bf16[16,4096]{0,1:T(8,128)(2,1)} %copy.15, bf16[16,4096]{0,1:T(8,128)(2,1)} %copy.16, ...), dimensions={0} | concatenate | bytes 8388608 | tf_op jit(solution)/shard_map/jit(_roll_dynamic)/concatenate | solution.py:59
  159.4 2.7 convert_multiply_fusion
  162.2 6.8 %fusion.11 = f32[256,64,64]{0,2,1:T(8,128)S(1)} fusion(f32[256,64,64]{0,2,1:T(8,128)S(1)} %bitcast.39), kind=kOutput, calls=%fused_computation.15 | convolution fusion | flops 805392384 | bytes 8388608 | tf_op jit(solution)/shard_map/ab,nbc,cd->nad/dot_general | solution.py:23
  169.0 6.1 %multiply_convert_fusion.1 = bf16[256,64,64]{0,2,1:T(8,128)(2,1)S(1)} fusion(f32[256,64,64]{0,2,1:T(8,128)S(1)} %fusion.11), kind=kOutput, calls=%fused_computation.17 | convolution fusion | flops 807489536 | bytes 6291456 | tf_op jit(solution)/shard_map/ab,nbc,cd->nad/dot_general | solution.py:23
  175.0 5.9 %fusion.2 = f32[256,1024]{1,0:T(8,128)S(1)} fusion(bf16[256,4096]{0,1:T(8,128)(2,1)S(1)} %bitcast.40, bf16[2,4096,1024]{2,1,0:T(8,128)(2,1)} %fusion), kind=kOutput, calls=%fused_computation.6 | convolution fusion | flops 2147483648 | bytes 11534336 | tf_op jit(solution)/shard_map/dot_general | solution.py:41
  181.0 2.4 fusion.19
  183.5 5.9 %fusion.3 = f32[256,1024]{1,0:T(8,128)S(1)} fusion(bf16[2,4096,1024]{2,1,0:T(8,128)(2,1)} %param.8, bf16[512,4096]{0,1:T(8,128)(2,1)S(1)} %copy-done, s32[]{:T(128)S(6)} %select_n.14), kind=kOutput, calls=%fused_computation.7 | convolution fusion | flops 2147483648 | bytes 11534340 | tf_op jit(solution)/shard_map/dot_general | solution.py:42
  189.3 13.5 %fusion.20 = f32[256,4096]{1,0:T(8,128)} fusion(bf16[1024,4096]{1,0:T(8,128)(2,1)} %param.11, bf16[256,1024]{1,0:T(8,128)(2,1)S(1)} %fusion.19, f32[256,1024]{1,0:T(8,128)S(1)} %fusion.3, bf16[2,4096,1024]{2,1,0:T(8,128)(2,1)} %param.8, bf16[512,4096]{0,1:T(8,128)(2,1)} %concatenate.6, s32[]{:T(128)S(6)} %select_n.14), kind=kOutput, calls=%fused_computation.26 | convolution fusion | flops 4297588736 | bytes 24641540 | tf_op jit(solution)/shard_map/dot_general | solution.py:66
  202.8 102.2 %all-reduce.1 = bf16[256,4096]{1,0:T(8,128)(2,1)S(1)} all-reduce(f32[256,4096]{1,0:T(8,128)} %fusion.20), channel_id=1, replica_groups=mesh['dom'=2,'tok'=16] {'tok'}, use_global_device_ids=true, to_apply=%region_0.1 | all-reduce | flops 1048576 | bytes 6291456 | tf_op jit(solution)/shard_map/psum | solution.py:67
  305.0 5.8 %multiply_convert_fusion = bf16[1024,4096]{1,0:T(8,128)(2,1)} fusion(bf16[256,1024]{1,0:T(8,128)(2,1)S(1)} %fusion.19, bf16[256,4096]{1,0:T(8,128)(2,1)S(1)} %all-reduce.1), kind=kOutput, calls=%fused_computation.2 | convolution fusion | flops 2155872256 | bytes 11010048 | tf_op jit(solution)/shard_map/dot_general | solution.py:68
  (68 shorter events, 15.1 us)
Async XLA Ops:
  0.0 4.9 %collective-permute-start = (bf16[16,4096]{1,0:T(8,128)(2,1)}, bf16[16,4096]{1,0:T(8,128)(2,1)S(1)}, u32[]{:S(2)}, u32[]{:S(2)}) collective-permute-start(bf16[16,4096]{1,0:T(8,128)(2,1)} %param.6), channel_id=1, source_target_pairs={{0,1},{1,2},{2,3},{3,4},{4,5},{5,6},{6,7},{7,8},{8,9},{9,10},{10,1... | collective-permute-start | bytes 393224 | tf_op jit(solution)/shard_map/ppermute | solution.py:55
  4.9 4.3 %collective-permute-start.1 = (bf16[16,4096]{1,0:T(8,128)(2,1)S(1)}, bf16[16,4096]{1,0:T(8,128)(2,1)S(1)}, u32[]{:S(2)}, u32[]{:S(2)}) collective-permute-start(bf16[16,4096]{1,0:T(8,128)(2,1)S(1)} %collective-permute-done), channel_id=1, source_target_pairs={{0,1},{1,2},{2,3},{3,4},{4,5},{5,6},{6,7},{7,8},{8,9},{9,10},{10,1... | collective-permute-start | bytes 393224 | tf_op jit(solution)/shard_map/ppermute | solution.py:55
  9.2 7.1 %collective-permute-start.2 = (bf16[16,4096]{1,0:T(8,128)(2,1)S(1)}, bf16[16,4096]{1,0:T(8,128)(2,1)S(1)}, u32[]{:S(2)}, u32[]{:S(2)}) collective-permute-start(bf16[16,4096]{1,0:T(8,128)(2,1)S(1)} %collective-permute-done.1), channel_id=1, source_target_pairs={{0,1},{1,2},{2,3},{3,4},{4,5},{5,6},{6,7},{7,8},{8,9},{9,10},{10,1... | collective-permute-start | bytes 393224 | tf_op jit(solution)/shard_map/ppermute | solution.py:55
  16.3 7.1 %collective-permute-start.3 = (bf16[16,4096]{1,0:T(8,128)(2,1)S(1)}, bf16[16,4096]{1,0:T(8,128)(2,1)S(1)}, u32[]{:S(2)}, u32[]{:S(2)}) collective-permute-start(bf16[16,4096]{1,0:T(8,128)(2,1)S(1)} %collective-permute-done.2), channel_id=1, source_target_pairs={{0,1},{1,2},{2,3},{3,4},{4,5},{5,6},{6,7},{7,8},{8,9},{9,10},{10,1... | collective-permute-start | bytes 393224 | tf_op jit(solution)/shard_map/ppermute | solution.py:55
  23.4 7.1 %collective-permute-start.4 = (bf16[16,4096]{1,0:T(8,128)(2,1)S(1)}, bf16[16,4096]{1,0:T(8,128)(2,1)S(1)}, u32[]{:S(2)}, u32[]{:S(2)}) collective-permute-start(bf16[16,4096]{1,0:T(8,128)(2,1)S(1)} %collective-permute-done.3), channel_id=1, source_target_pairs={{0,1},{1,2},{2,3},{3,4},{4,5},{5,6},{6,7},{7,8},{8,9},{9,10},{10,1... | collective-permute-start | bytes 393224 | tf_op jit(solution)/shard_map/ppermute | solution.py:55
  30.5 72.6 %copy-start.1 = (bf16[16,4096]{1,0:T(8,128)(2,1)}, bf16[16,4096]{1,0:T(8,128)(2,1)S(1)}, u32[]{:S(2)}) copy-start(bf16[16,4096]{1,0:T(8,128)(2,1)S(1)} %collective-permute-done.4) | copy-start | bytes 393220
  30.5 7.1 %collective-permute-start.5 = (bf16[16,4096]{1,0:T(8,128)(2,1)S(1)}, bf16[16,4096]{1,0:T(8,128)(2,1)S(1)}, u32[]{:S(2)}, u32[]{:S(2)}) collective-permute-start(bf16[16,4096]{1,0:T(8,128)(2,1)S(1)} %collective-permute-done.4), channel_id=1, source_target_pairs={{0,1},{1,2},{2,3},{3,4},{4,5},{5,6},{6,7},{7,8},{8,9},{9,10},{10,1... | collective-permute-start | bytes 393224 | tf_op jit(solution)/shard_map/ppermute | solution.py:55
  37.6 65.5 %copy-start.2 = (bf16[16,4096]{1,0:T(8,128)(2,1)}, bf16[16,4096]{1,0:T(8,128)(2,1)S(1)}, u32[]{:S(2)}) copy-start(bf16[16,4096]{1,0:T(8,128)(2,1)S(1)} %collective-permute-done.5) | copy-start | bytes 393220
  37.6 7.1 %collective-permute-start.6 = (bf16[16,4096]{1,0:T(8,128)(2,1)S(1)}, bf16[16,4096]{1,0:T(8,128)(2,1)S(1)}, u32[]{:S(2)}, u32[]{:S(2)}) collective-permute-start(bf16[16,4096]{1,0:T(8,128)(2,1)S(1)} %collective-permute-done.5), channel_id=1, source_target_pairs={{0,1},{1,2},{2,3},{3,4},{4,5},{5,6},{6,7},{7,8},{8,9},{9,10},{10,1... | collective-permute-start | bytes 393224 | tf_op jit(solution)/shard_map/ppermute | solution.py:55
  44.7 58.4 %copy-start.3 = (bf16[16,4096]{1,0:T(8,128)(2,1)}, bf16[16,4096]{1,0:T(8,128)(2,1)S(1)}, u32[]{:S(2)}) copy-start(bf16[16,4096]{1,0:T(8,128)(2,1)S(1)} %collective-permute-done.6) | copy-start | bytes 393220
  44.7 7.1 %collective-permute-start.7 = (bf16[16,4096]{1,0:T(8,128)(2,1)S(1)}, bf16[16,4096]{1,0:T(8,128)(2,1)S(1)}, u32[]{:S(2)}, u32[]{:S(2)}) collective-permute-start(bf16[16,4096]{1,0:T(8,128)(2,1)S(1)} %collective-permute-done.6), channel_id=1, source_target_pairs={{0,1},{1,2},{2,3},{3,4},{4,5},{5,6},{6,7},{7,8},{8,9},{9,10},{10,1... | collective-permute-start | bytes 393224 | tf_op jit(solution)/shard_map/ppermute | solution.py:55
  51.7 51.3 %copy-start.5 = (bf16[16,4096]{1,0:T(8,128)(2,1)}, bf16[16,4096]{1,0:T(8,128)(2,1)S(1)}, u32[]{:S(2)}) copy-start(bf16[16,4096]{1,0:T(8,128)(2,1)S(1)} %collective-permute-done.7) | copy-start | bytes 393220
  51.7 7.1 %collective-permute-start.8 = (bf16[16,4096]{1,0:T(8,128)(2,1)S(1)}, bf16[16,4096]{1,0:T(8,128)(2,1)S(1)}, u32[]{:S(2)}, u32[]{:S(2)}) collective-permute-start(bf16[16,4096]{1,0:T(8,128)(2,1)S(1)} %collective-permute-done.7), channel_id=1, source_target_pairs={{0,1},{1,2},{2,3},{3,4},{4,5},{5,6},{6,7},{7,8},{8,9},{9,10},{10,1... | collective-permute-start | bytes 393224 | tf_op jit(solution)/shard_map/ppermute | solution.py:55
  58.8 44.2 %copy-start.7 = (bf16[16,4096]{1,0:T(8,128)(2,1)}, bf16[16,4096]{1,0:T(8,128)(2,1)S(1)}, u32[]{:S(2)}) copy-start(bf16[16,4096]{1,0:T(8,128)(2,1)S(1)} %collective-permute-done.8) | copy-start | bytes 393220
  58.8 7.1 %collective-permute-start.9 = (bf16[16,4096]{1,0:T(8,128)(2,1)S(1)}, bf16[16,4096]{1,0:T(8,128)(2,1)S(1)}, u32[]{:S(2)}, u32[]{:S(2)}) collective-permute-start(bf16[16,4096]{1,0:T(8,128)(2,1)S(1)} %collective-permute-done.8), channel_id=1, source_target_pairs={{0,1},{1,2},{2,3},{3,4},{4,5},{5,6},{6,7},{7,8},{8,9},{9,10},{10,1... | collective-permute-start | bytes 393224 | tf_op jit(solution)/shard_map/ppermute | solution.py:55
  65.9 37.1 %copy-start.9 = (bf16[16,4096]{1,0:T(8,128)(2,1)}, bf16[16,4096]{1,0:T(8,128)(2,1)S(1)}, u32[]{:S(2)}) copy-start(bf16[16,4096]{1,0:T(8,128)(2,1)S(1)} %collective-permute-done.9) | copy-start | bytes 393220
  65.9 7.1 %collective-permute-start.10 = (bf16[16,4096]{1,0:T(8,128)(2,1)S(1)}, bf16[16,4096]{1,0:T(8,128)(2,1)S(1)}, u32[]{:S(2)}, u32[]{:S(2)}) collective-permute-start(bf16[16,4096]{1,0:T(8,128)(2,1)S(1)} %collective-permute-done.9), channel_id=1, source_target_pairs={{0,1},{1,2},{2,3},{3,4},{4,5},{5,6},{6,7},{7,8},{8,9},{9,10},{10,1... | collective-permute-start | bytes 393224 | tf_op jit(solution)/shard_map/ppermute | solution.py:55
  73.0 30.0 %copy-start.10 = (bf16[16,4096]{1,0:T(8,128)(2,1)}, bf16[16,4096]{1,0:T(8,128)(2,1)S(1)}, u32[]{:S(2)}) copy-start(bf16[16,4096]{1,0:T(8,128)(2,1)S(1)} %collective-permute-done.10) | copy-start | bytes 393220
  73.0 7.1 %collective-permute-start.11 = (bf16[16,4096]{1,0:T(8,128)(2,1)S(1)}, bf16[16,4096]{1,0:T(8,128)(2,1)S(1)}, u32[]{:S(2)}, u32[]{:S(2)}) collective-permute-start(bf16[16,4096]{1,0:T(8,128)(2,1)S(1)} %collective-permute-done.10), channel_id=1, source_target_pairs={{0,1},{1,2},{2,3},{3,4},{4,5},{5,6},{6,7},{7,8},{8,9},{9,10},{10,1... | collective-permute-start | bytes 393224 | tf_op jit(solution)/shard_map/ppermute | solution.py:55
  80.1 23.0 %copy-start.11 = (bf16[16,4096]{1,0:T(8,128)(2,1)}, bf16[16,4096]{1,0:T(8,128)(2,1)S(1)}, u32[]{:S(2)}) copy-start(bf16[16,4096]{1,0:T(8,128)(2,1)S(1)} %collective-permute-done.11) | copy-start | bytes 393220
  80.1 7.1 %collective-permute-start.12 = (bf16[16,4096]{1,0:T(8,128)(2,1)S(1)}, bf16[16,4096]{1,0:T(8,128)(2,1)S(1)}, u32[]{:S(2)}, u32[]{:S(2)}) collective-permute-start(bf16[16,4096]{1,0:T(8,128)(2,1)S(1)} %collective-permute-done.11), channel_id=1, source_target_pairs={{0,1},{1,2},{2,3},{3,4},{4,5},{5,6},{6,7},{7,8},{8,9},{9,10},{10,1... | collective-permute-start | bytes 393224 | tf_op jit(solution)/shard_map/ppermute | solution.py:55
  87.2 15.9 %copy-start.13 = (bf16[16,4096]{1,0:T(8,128)(2,1)}, bf16[16,4096]{1,0:T(8,128)(2,1)S(1)}, u32[]{:S(2)}) copy-start(bf16[16,4096]{1,0:T(8,128)(2,1)S(1)} %collective-permute-done.12) | copy-start | bytes 393220
  87.2 15.9 %collective-permute-start.13 = (bf16[16,4096]{1,0:T(8,128)(2,1)S(1)}, bf16[16,4096]{1,0:T(8,128)(2,1)}, u32[]{:S(2)}, u32[]{:S(2)}) collective-permute-start(bf16[16,4096]{1,0:T(8,128)(2,1)S(1)} %collective-permute-done.12), channel_id=1, source_target_pairs={{0,1},{1,2},{2,3},{3,4},{4,5},{5,6},{6,7},{7,8},{8,9},{9,10},{10,1... | collective-permute-start | bytes 393224 | tf_op jit(solution)/shard_map/ppermute | solution.py:55
  88.3 14.9 %copy-start.15 = (s32[4096]{0:T(1024)S(1)}, s32[4096]{0:T(1024)}, u32[]{:S(2)}) copy-start(s32[4096]{0:T(1024)} %param.7) | copy-start | bytes 49156
  103.1 21.8 %collective-permute-start.14 = (bf16[16,4096]{1,0:T(8,128)(2,1)}, bf16[16,4096]{1,0:T(8,128)(2,1)}, u32[]{:S(2)}, u32[]{:S(2)}) collective-permute-start(bf16[16,4096]{1,0:T(8,128)(2,1)} %collective-permute-done.13), channel_id=1, source_target_pairs={{0,1},{1,2},{2,3},{3,4},{4,5},{5,6},{6,7},{7,8},{8,9},{9,10},{10,1... | collective-permute-start | bytes 393224 | tf_op jit(solution)/shard_map/ppermute | solution.py:55
  104.2 7.1 %copy-start.4 = (bf16[16,4096]{1,0:T(8,128)(2,1)S(1)}, bf16[16,4096]{1,0:T(8,128)(2,1)}, u32[]{:S(2)}) copy-start(bf16[16,4096]{1,0:T(8,128)(2,1)} %copy-done.3) | copy-start | bytes 393220
  105.5 7.2 %copy-start.6 = (bf16[16,4096]{1,0:T(8,128)(2,1)S(1)}, bf16[16,4096]{1,0:T(8,128)(2,1)}, u32[]{:S(2)}) copy-start(bf16[16,4096]{1,0:T(8,128)(2,1)} %copy-done.5) | copy-start | bytes 393220
  106.8 7.2 %copy-start.8 = (bf16[16,4096]{1,0:T(8,128)(2,1)S(1)}, bf16[16,4096]{1,0:T(8,128)(2,1)}, u32[]{:S(2)}) copy-start(bf16[16,4096]{1,0:T(8,128)(2,1)} %copy-done.7) | copy-start | bytes 393220
  112.7 7.3 %copy-start.12 = (bf16[16,4096]{1,0:T(8,128)(2,1)S(1)}, bf16[16,4096]{1,0:T(8,128)(2,1)}, u32[]{:S(2)}) copy-start(bf16[16,4096]{1,0:T(8,128)(2,1)} %copy-done.11) | copy-start | bytes 393220
  114.0 7.3 %copy-start.14 = (bf16[16,4096]{1,0:T(8,128)(2,1)S(1)}, bf16[16,4096]{1,0:T(8,128)(2,1)}, u32[]{:S(2)}) copy-start(bf16[16,4096]{1,0:T(8,128)(2,1)} %copy-done.13) | copy-start | bytes 393220
  162.2 18.8 %slice-start = ((s8[16777216]{0:T(1024)(128)(4,1)}), s8[4194304]{0:T(1024)(128)(4,1)S(1)}, s32[]{:S(2)}) async-start(s8[16777216]{0:T(1024)(128)(4,1)} %bitcast.37), calls=%async_computation | async-start | bytes 8388608
  162.2 18.8 %slice-start.1 = ((s8[16777216]{0:T(1024)(128)(4,1)}), s8[4194304]{0:T(1024)(128)(4,1)S(1)}, s32[]{:S(2)}) async-start(s8[16777216]{0:T(1024)(128)(4,1)} %bitcast.37), calls=%async_computation.1 | async-start | bytes 8388608
  (3 other events, 14.3 us)
